TPU v7x, 128 devices: a whole 4x4x4 slice. The times are simulated.
128 devices in a mesh: expert: 32 (over x, y, core), tensor: 4 (over z).
Axes of the slice: x: 4, y: 4, z: 4, core: 2. Of those that a mesh axis runs over, the one named last changes fastest.
Arguments:
- tokens: bfloat16 [65536, 512], P(('expert', 'tensor')), may hold values from -6 to 6
- first_gain: float32 [512], replicated, may hold values from 0.5 to 1.5
- second_gain: float32 [512], replicated, may hold values from 0.5 to 1.5
- query_weight: bfloat16 [512, 512], P(None, 'tensor'), may hold values from -0.25 to 0.25
- key_weight: bfloat16 [512, 512], P(None, 'tensor'), may hold values from -0.25 to 0.25
- value_weight: bfloat16 [512, 512], P(None, 'tensor'), may hold values from -0.25 to 0.25
- output_weight: bfloat16 [512, 512], P('tensor'), may hold values from -2 to 2
- router_weight: bfloat16 [512, 32], replicated, may hold values from -0.125 to 0.125
- expert_in: bfloat16 [32, 512, 2048], P('expert', None, 'tensor'), may hold values from -0.5 to 0.5
- expert_out: bfloat16 [32, 2048, 512], P('expert', 'tensor'), may hold values from -0.5 to 0.5
- cotangent: float32 [65536, 512], P(('expert', 'tensor')), may hold values from -6 to 6
- routes: int32 [65536, 4], P(('expert', 'tensor')), may hold values from 0 to 31, all different within a row
- priority: int32 [2048, 32], P(('expert', 'tensor')), may hold values from 0 to 31, each once within a row
- prefix_len: int32 [32], P('expert'), may hold values from 204 to 1024
Outputs:
- layer_output: bfloat16 [65536, 512], P(('expert', 'tensor'))
- tokens_grad: float32 [65536, 512], P(('expert', 'tensor'))
- first_gain_grad: float32 [512], replicated
- second_gain_grad: float32 [512], replicated
- query_grad: float32 [512, 512], P(None, 'tensor')
- key_grad: float32 [512, 512], P(None, 'tensor')
- value_grad: float32 [512, 512], P(None, 'tensor')
- output_grad: float32 [512, 512], P('tensor')
- router_grad: float32 [512, 32], replicated
- expert_in_grad: float32 [32, 512, 2048], P('expert', None, 'tensor')
- expert_out_grad: float32 [32, 2048, 512], P('expert', 'tensor')
Inputs may be any that keep to these rules, and one draw needn't show every extreme that they name: `routes`: each row names 4 different experts, and every expert is named by some row. `priority`: each row holds every number of 0 to 31 once.
All inputs are finite; a program needn't handle non-finite values.
Results may differ from a plain program's by a relative error of at most 0.028.
Values may be sent and summed in bfloat16 or wider, within the bound.
A program may use at most 128 MiB of HBM per device.

v0:
```python
import jax
import jax.numpy as jnp
from jax import lax
from jax.sharding import PartitionSpec as P

HEAD_DIM = 64
GROUP = 32
TOP = 4
EPS = 1e-05
NEG = -1e30


def norm_rows(values, gain_vec):
    center = values - jnp.mean(values, axis=-1, keepdims=True)
    spread = lax.rsqrt(jnp.mean(center * center, axis=-1, keepdims=True) + EPS)
    scaled = center * spread
    return (scaled, spread, scaled * gain_vec)


def norm_back(grad_in, scaled, spread, gain_vec):
    grad_scaled = grad_in * gain_vec
    centered = grad_scaled - jnp.mean(grad_scaled, axis=-1, keepdims=True)
    return spread * (centered - scaled * jnp.mean(grad_scaled * scaled, axis=-1, keepdims=True))


def block_scores(queries, key_rows, start_row, block_rows, prefix):
    query_blk = lax.dynamic_slice_in_dim(queries, start_row, block_rows, 0)
    scores = jnp.einsum(
        "qhd,khd->hqk", query_blk, key_rows, preferred_element_type=jnp.float32
    ) * HEAD_DIM ** (-0.5)
    row_ids = start_row + jnp.arange(block_rows, dtype=jnp.int32)
    col_ids = jnp.arange(key_rows.shape[0], dtype=jnp.int32)
    allowed = (col_ids[None, :] <= row_ids[:, None]) | (col_ids[None, :] < prefix)
    return (query_blk, jnp.where(allowed[None], scores, NEG))


def attend_forward(queries, key_rows, value_rows, prefix, block_rows):
    length = key_rows.shape[0]

    def one_block(start_row):
        query_blk, scores = block_scores(queries, key_rows, start_row, block_rows, prefix)
        row_peak = jnp.max(scores, axis=-1, keepdims=True)
        exp_scores = jnp.exp(scores - row_peak)
        exp_total = jnp.sum(exp_scores, axis=-1, keepdims=True)
        soft_rows = (exp_scores / exp_total).astype(jnp.bfloat16)
        context = jnp.einsum(
            "hqk,khd->qhd", soft_rows, value_rows, preferred_element_type=jnp.float32
        )
        return (context.astype(jnp.bfloat16), (row_peak + jnp.log(exp_total))[..., 0])

    starts = jnp.arange(length // block_rows, dtype=jnp.int32) * block_rows
    context, log_total = lax.map(one_block, starts)
    return (context.reshape(length, queries.shape[1] * queries.shape[2]), log_total)


def attend_backward(queries, key_rows, value_rows, grad_context, log_total, prefix, block_rows):
    length = key_rows.shape[0]
    score_scale = HEAD_DIM ** (-0.5)

    def one_block(carried, inputs):
        grad_keys, grad_values = carried
        start_row, block_log = inputs
        query_blk, scores = block_scores(queries, key_rows, start_row, block_rows, prefix)
        soft_rows = jnp.exp(scores - block_log[..., None])
        grad_blk = lax.dynamic_slice_in_dim(grad_context, start_row, block_rows, 0)
        grad_soft = jnp.einsum(
            "qhd,khd->hqk", grad_blk, value_rows, preferred_element_type=jnp.float32
        )
        inner_sum = jnp.sum(soft_rows * grad_soft, axis=-1, keepdims=True)
        grad_scores = (soft_rows * (grad_soft - inner_sum)).astype(jnp.bfloat16)
        grad_values = grad_values + jnp.einsum(
            "hqk,qhd->khd",
            soft_rows.astype(jnp.bfloat16),
            grad_blk,
            preferred_element_type=jnp.float32,
        )
        grad_keys = grad_keys + score_scale * jnp.einsum(
            "hqk,qhd->khd", grad_scores, query_blk, preferred_element_type=jnp.float32
        )
        grad_query = score_scale * jnp.einsum(
            "hqk,khd->qhd", grad_scores, key_rows, preferred_element_type=jnp.float32
        )
        return ((grad_keys, grad_values), grad_query)

    empty_rows = jnp.zeros(key_rows.shape, jnp.float32)
    starts = jnp.arange(length // block_rows, dtype=jnp.int32) * block_rows
    (grad_keys, grad_values), grad_query = lax.scan(
        one_block, (empty_rows, empty_rows), (starts, log_total)
    )
    return (
        grad_query.reshape(length, -1),
        grad_keys.reshape(length, -1),
        grad_values.reshape(length, -1),
    )


def to_homes(part_out, expert_size):
    local_experts, row_total, width = part_out.shape
    moved = part_out.reshape(local_experts, expert_size, -1, width).transpose(1, 0, 2, 3)
    return moved.reshape(expert_size * local_experts, -1, width)


def body(
    tokens,
    first_gain,
    second_gain,
    query_weight,
    key_weight,
    value_weight,
    output_weight,
    router_weight,
    expert_in,
    expert_out,
    cotangent,
    routes,
    priority,
    prefix_len,
):
    row_count, width = tokens.shape
    tensor_size = lax.axis_size("tensor")
    expert_size = lax.axis_size("expert")
    length = row_count * tensor_size
    block_rows = min(512, length)
    head_count = query_weight.shape[1] // HEAD_DIM
    experts = router_weight.shape[1]
    groups = row_count // GROUP
    capacity = (5 * GROUP * TOP + 4 * experts - 1) // (4 * experts)
    prefix = prefix_len[0]
    stream = tokens.astype(jnp.float32)
    scaled_one, spread_one, normed_one = norm_rows(stream, first_gain)
    sequence = lax.all_gather(normed_one.astype(jnp.bfloat16), "tensor", axis=0, tiled=True)
    queries = jnp.dot(sequence, query_weight, preferred_element_type=jnp.float32).astype(
        jnp.bfloat16
    )
    key_rows = jnp.dot(sequence, key_weight, preferred_element_type=jnp.float32).astype(
        jnp.bfloat16
    )
    value_rows = jnp.dot(sequence, value_weight, preferred_element_type=jnp.float32).astype(
        jnp.bfloat16
    )
    query_heads = queries.reshape(length, head_count, HEAD_DIM)
    key_heads = key_rows.reshape(length, head_count, HEAD_DIM)
    value_heads = value_rows.reshape(length, head_count, HEAD_DIM)
    context, log_total = attend_forward(query_heads, key_heads, value_heads, prefix, block_rows)
    attended = lax.psum_scatter(
        jnp.dot(context, output_weight, preferred_element_type=jnp.float32).astype(jnp.bfloat16),
        "tensor",
        scatter_dimension=0,
        tiled=True,
    ).astype(jnp.float32)
    residual = stream + attended
    scaled_two, spread_two, normed_two = norm_rows(residual, second_gain)
    mixer_in = normed_two.astype(jnp.bfloat16)
    logits = jnp.dot(mixer_in, router_weight, preferred_element_type=jnp.float32)
    member = jnp.sum(
        (routes[:, :, None] == jnp.arange(experts, dtype=jnp.int32)).astype(jnp.float32), axis=1
    )
    member = member.reshape(groups, GROUP, experts)
    earlier = (priority[:, :, None] < priority[:, None, :]).astype(jnp.float32)
    order_rank = jnp.einsum("gst,gse->gte", earlier, member)
    kept_pairs = member * (order_rank < capacity).astype(jnp.float32)
    exp_terms = kept_pairs * jnp.exp(logits.reshape(groups, GROUP, experts))
    exp_total = jnp.sum(exp_terms, axis=1, keepdims=True)
    kept_count = jnp.sum(kept_pairs, axis=1, keepdims=True)
    weights = exp_terms / jnp.where(kept_count > 0, exp_total, 1.0)
    weights_low = weights.astype(jnp.bfloat16)
    grouped = mixer_in.reshape(groups, GROUP, width)
    mixed_rows = jnp.einsum(
        "gte,gtd->egd", weights_low, grouped, preferred_element_type=jnp.float32
    ).astype(jnp.bfloat16)
    sequence_mix = lax.all_gather(mixed_rows, "tensor", axis=1, tiled=True)
    owner_rows = lax.all_to_all(sequence_mix, "expert", split_axis=0, concat_axis=1, tiled=True)
    hidden_pre = jnp.einsum(
        "erd,edf->erf", owner_rows, expert_in, preferred_element_type=jnp.float32
    )
    sigma_pre = jax.nn.sigmoid(hidden_pre)
    hidden = (hidden_pre * sigma_pre).astype(jnp.bfloat16)
    part_out = jnp.einsum("erf,efd->erd", hidden, expert_out, preferred_element_type=jnp.float32)
    arrived = lax.all_to_all(
        to_homes(part_out, expert_size).astype(jnp.bfloat16),
        "expert",
        split_axis=0,
        concat_axis=0,
        tiled=True,
    )
    summed = lax.psum_scatter(arrived, "tensor", scatter_dimension=1, tiled=True).astype(
        jnp.float32
    )
    returned = summed.astype(jnp.bfloat16)
    mixed_back = jnp.einsum(
        "gte,egd->gtd", weights_low, returned, preferred_element_type=jnp.float32
    ).reshape(row_count, width)
    layer_output = (residual + mixed_back).astype(jnp.bfloat16)
    grad_mix = cotangent.astype(jnp.bfloat16).reshape(groups, GROUP, width)
    grad_returned = jnp.einsum(
        "gte,gtd->egd", weights_low, grad_mix, preferred_element_type=jnp.float32
    ).astype(jnp.bfloat16)
    grad_weights = jnp.einsum(
        "gtd,egd->gte", grad_mix, returned, preferred_element_type=jnp.float32
    )
    sequence_grad = lax.all_gather(grad_returned, "tensor", axis=1, tiled=True)
    grad_owner = lax.all_to_all(sequence_grad, "expert", split_axis=0, concat_axis=1, tiled=True)
    grad_hidden = jnp.einsum(
        "erd,efd->erf", grad_owner, expert_out, preferred_element_type=jnp.float32
    )
    slope = sigma_pre * (1.0 + hidden_pre * (1.0 - sigma_pre))
    grad_pre = (grad_hidden * slope).astype(jnp.bfloat16)
    expert_out_grad = jnp.einsum(
        "erf,erd->efd", hidden, grad_owner, preferred_element_type=jnp.float32
    )
    expert_in_grad = jnp.einsum(
        "erd,erf->edf", owner_rows, grad_pre, preferred_element_type=jnp.float32
    )
    grad_part = jnp.einsum("erf,edf->erd", grad_pre, expert_in, preferred_element_type=jnp.float32)
    grad_arrived = lax.all_to_all(
        to_homes(grad_part, expert_size).astype(jnp.bfloat16),
        "expert",
        split_axis=0,
        concat_axis=0,
        tiled=True,
    )
    grad_summed = lax.psum_scatter(grad_arrived, "tensor", scatter_dimension=1, tiled=True).astype(
        jnp.float32
    )
    grad_mixed = grad_summed.astype(jnp.bfloat16)
    grad_grouped = jnp.einsum(
        "gte,egd->gtd", weights_low, grad_mixed, preferred_element_type=jnp.float32
    )
    grad_weights = grad_weights + jnp.einsum(
        "egd,gtd->gte", grad_mixed, grouped, preferred_element_type=jnp.float32
    )
    inner_sum = jnp.sum(weights * grad_weights, axis=1, keepdims=True)
    grad_logits = (
        (weights * (grad_weights - inner_sum)).reshape(row_count, experts).astype(jnp.bfloat16)
    )
    router_part = jnp.einsum("td,te->de", mixer_in, grad_logits, preferred_element_type=jnp.float32)
    grad_mixer = grad_grouped.reshape(row_count, width) + jnp.einsum(
        "te,de->td", grad_logits, router_weight, preferred_element_type=jnp.float32
    )
    second_part = jnp.sum(grad_mixer * scaled_two, axis=0)
    grad_residual = cotangent + norm_back(grad_mixer, scaled_two, spread_two, second_gain)
    grad_sequence = lax.all_gather(grad_residual.astype(jnp.bfloat16), "tensor", axis=0, tiled=True)
    output_part = jnp.einsum(
        "lc,ld->cd", context, grad_sequence, preferred_element_type=jnp.float32
    )
    grad_context = jnp.einsum(
        "ld,cd->lc", grad_sequence, output_weight, preferred_element_type=jnp.float32
    ).astype(jnp.bfloat16)
    grad_query, grad_keys, grad_values = attend_backward(
        query_heads,
        key_heads,
        value_heads,
        grad_context.reshape(length, head_count, HEAD_DIM),
        log_total,
        prefix,
        block_rows,
    )
    grad_query = grad_query.astype(jnp.bfloat16)
    grad_keys = grad_keys.astype(jnp.bfloat16)
    grad_values = grad_values.astype(jnp.bfloat16)
    query_part = jnp.einsum("ld,lc->dc", sequence, grad_query, preferred_element_type=jnp.float32)
    key_part = jnp.einsum("ld,lc->dc", sequence, grad_keys, preferred_element_type=jnp.float32)
    value_part = jnp.einsum("ld,lc->dc", sequence, grad_values, preferred_element_type=jnp.float32)
    total_grad = jnp.einsum(
        "lc,dc->ld", grad_query, query_weight, preferred_element_type=jnp.float32
    )
    total_grad = total_grad + jnp.einsum(
        "lc,dc->ld", grad_keys, key_weight, preferred_element_type=jnp.float32
    )
    grad_normed = lax.psum_scatter(
        (
            total_grad
            + jnp.einsum("lc,dc->ld", grad_values, value_weight, preferred_element_type=jnp.float32)
        ).astype(jnp.bfloat16),
        "tensor",
        scatter_dimension=0,
        tiled=True,
    ).astype(jnp.float32)
    first_part = jnp.sum(grad_normed * scaled_one, axis=0)
    tokens_grad = grad_residual + norm_back(grad_normed, scaled_one, spread_one, first_gain)
    query_grad, key_grad, value_grad, output_grad = (
        lax.psum(query_part.astype(jnp.bfloat16), "expert").astype(jnp.float32),
        lax.psum(key_part.astype(jnp.bfloat16), "expert").astype(jnp.float32),
        lax.psum(value_part.astype(jnp.bfloat16), "expert").astype(jnp.float32),
        lax.psum(output_part.astype(jnp.bfloat16), "expert").astype(jnp.float32),
    )
    first_gain_grad, second_gain_grad, router_grad = lax.psum(
        (first_part, second_part, router_part), ("expert", "tensor")
    )
    return (
        layer_output,
        tokens_grad,
        first_gain_grad,
        second_gain_grad,
        query_grad,
        key_grad,
        value_grad,
        output_grad,
        router_grad,
        expert_in_grad,
        expert_out_grad,
    )


def solution(mesh):
    in_specs = (
        P(("expert", "tensor"), None),
        P(),
        P(),
        P(None, "tensor"),
        P(None, "tensor"),
        P(None, "tensor"),
        P("tensor", None),
        P(),
        P("expert", None, "tensor"),
        P("expert", "tensor", None),
        P(("expert", "tensor"), None),
        P(("expert", "tensor"), None),
        P(("expert", "tensor"), None),
        P("expert"),
    )
    out_specs = (
        P(("expert", "tensor"), None),
        P(("expert", "tensor"), None),
        P(),
        P(),
        P(None, "tensor"),
        P(None, "tensor"),
        P(None, "tensor"),
        P("tensor", None),
        P(),
        P("expert", None, "tensor"),
        P("expert", "tensor", None),
    )
    return jax.shard_map(body, mesh=mesh, in_specs=in_specs, out_specs=out_specs, check_vma=False)
```

profile of v0, /device:TPU:1, one launch (start us, length us, event | category | flops | bytes accessed | tf_op | source)
XLA Modules:
  0.0 777.5 jit_solution(236218361544068434)
XLA Ops:
  12.6 33.8 %all-gather.5.cloned.1.call-done = bf16[2048,512]{1,0:T(8,128)(2,1)} async-done(((bf16[512,512]{1,0:T(8,128)(2,1)}), bf16[2048,512]{1,0:T(8,128)(2,1)}) %all-gather.5.cloned.1.call-update) | async-done | bytes 2097168 | tf_op jit(solution)/shard_map/all_gather | solution.py:131
  53.1 56.4 %while.27 = (s32[]{:T(128)}, bf16[4,512,2,64]{1,3,2,0:T(8,128)(2,1)S(1)}, f32[4,2,512]{2,1,0:T(2,128)}, s32[4]{0:T(128)}, s32[]{:T(128)}, /*index=5*/bf16[2048,2...) while((s32[]{:T(128)}, ...), condition=%wide.region_5.6_spmd, body=%wide.region_2.5_spmd.sunk | while | flops 564200960 | bytes 30711992 | solution.py:52
  58.4 3.1 fusion.162
  72.5 3.1 fusion.162
  86.6 3.0 fusion.162
  113.2 29.8 %reduce-scatter.5.cloned.1.call-done = bf16[512,512]{1,0:T(8,128)(2,1)} async-done(((bf16[2048,512]{1,0:T(8,128)(2,1)}), bf16[512,512]{1,0:T(8,128)(2,1)}) %reduce-scatter.5.cloned.1.call-update) | async-done | bytes 524304 | tf_op jit(solution)/shard_map/reduce_scatter | solution.py:145
  151.3 28.2 %all-gather.7.cloned.1.call-done = bf16[32,64,512]{2,0,1:T(8,128)(2,1)} async-done(((bf16[32,16,512]{2,0,1:T(8,128)(2,1)}), bf16[32,64,512]{2,0,1:T(8,128)(2,1)}) %all-gather.7.cloned.1.call-update) | async-done | bytes 2097168 | tf_op jit(solution)/shard_map/all_gather | solution.py:171
  179.5 4.1 copy.64
  183.6 8.1 %all-to-all-start = ((bf16[32,64,512]{2,1,0:T(8,128)(2,1)}), bf16[32,64,512]{2,1,0:T(8,128)(2,1)}, u32[]{:S(2)}, u32[]{:S(2)}) async-start(bf16[32,64,512]{2,1,0:T(8,128)(2,1)} %copy.64), calls=%async_computation.1 | async-start | bytes 4194304 | tf_op jit(solution)/shard_map/all_to_all | solution.py:172
  191.7 21.0 %all-gather.9.cloned.1.call-done = bf16[32,64,512]{2,0,1:T(8,128)(2,1)} async-done(((bf16[32,16,512]{2,0,1:T(8,128)(2,1)}), bf16[32,64,512]{2,0,1:T(8,128)(2,1)}) %all-gather.9.cloned.1.call-update) | async-done | bytes 2097168 | tf_op jit(solution)/shard_map/all_gather | solution.py:201
  212.7 4.1 copy.67
  216.8 3.2 all-to-all-done
  220.0 5.2 all-to-all-start.2
  225.3 6.0 multiply_convert_fusion.2
  231.3 22.4 %all-to-all-done.2 = bf16[32,64,512]{2,1,0:T(8,128)(2,1)} async-done(((bf16[32,64,512]{2,1,0:T(8,128)(2,1)}), bf16[32,64,512]{2,1,0:T(8,128)(2,1)}, u32[]{:S(2)}, u32[]{:S(2)}) %all-to-all-start.2) | async-done | bytes 2097184 | tf_op jit(solution)/shard_map/all_to_all | solution.py:202
  253.7 5.2 multiply_convert_fusion.1
  261.6 32.6 %all_to_all.28 = bf16[32,64,512]{2,1,0:T(8,128)(2,1)} all-to-all(bf16[32,64,512]{2,1,0:T(8,128)(2,1)S(1)} %convolution_convert_fusion.5), channel_id=1, replica_groups=mesh['expert'=32,'tensor'=4] {'expert'}, dimensions={0} | all-to-all | bytes 4194304 | tf_op jit(solution)/shard_map/all_to_all | solution.py:215
  297.1 32.0 %all_to_all.29 = bf16[32,64,512]{2,1,0:T(8,128)(2,1)} all-to-all(bf16[32,64,512]{2,1,0:T(8,128)(2,1)S(1)} %convolution_convert_fusion.6), channel_id=1, replica_groups=mesh['expert'=32,'tensor'=4] {'expert'}, dimensions={0} | all-to-all | bytes 4194304 | tf_op jit(solution)/shard_map/all_to_all | solution.py:179
  331.5 24.1 %reduce-scatter.7.cloned.1.call-done = bf16[32,16,512]{2,1,0:T(8,128)(2,1)} async-done(((bf16[32,64,512]{2,1,0:T(8,128)(2,1)}), bf16[32,16,512]{2,1,0:T(8,128)(2,1)}) %reduce-scatter.7.cloned.1.call-update) | async-done | bytes 524304 | tf_op jit(solution)/shard_map/reduce_scatter | solution.py:186
  362.9 30.5 %all-gather.11.cloned.1.call-done = bf16[2048,512]{1,0:T(8,128)(2,1)} async-done(((bf16[512,512]{1,0:T(8,128)(2,1)}), bf16[2048,512]{1,0:T(8,128)(2,1)}) %all-gather.11.cloned.1.call-update) | async-done | bytes 2097168 | tf_op jit(solution)/shard_map/all_gather | solution.py:242
  395.8 81.7 %while.28 = (s32[]{:T(128)}, f32[2048,2,64]{0,2,1:T(8,128)S(1)}, f32[2048,2,64]{0,2,1:T(8,128)}, bf16[4,512,2,64]{1,3,2,0:T(8,128)(2,1)}, s32[4]{0:T(128)}, /*in...) while((s32[]{:T(128)}, f32[2048,2,64]{0,2,1:T(8,128)S(1)}, ...), condition=%wide.region_19.20_spmd.clone, body=%wide.region_17.19_spmd.clone.sunk | while | flops 1377109504 | bytes 86282592 | solution.py:87
  406.8 3.2 multiply_reduce_fusion.7
  427.2 3.2 multiply_reduce_fusion.7
  447.6 3.2 multiply_reduce_fusion.7
  468.0 3.2 multiply_reduce_fusion.7
  490.3 5.5 add_convert_fusion
  495.9 4.6 convolution_bitcast_fusion
  500.6 4.0 convolution_bitcast_fusion.1
  505.5 88.3 %all-reduce.7.cloned.1.call-done = (bf16[512,128]{1,0:T(8,128)(2,1)}, bf16[512,128]{1,0:T(8,128)(2,1)}, bf16[512,128]{1,0:T(8,128)(2,1)}, bf16[128,512]{1,0:T(8,128)(2,1)}) async-done(((bf16[512,128]{1,0:T(8,128)(2,1)}, bf16[512,128]{1,0:T(8,128)(2,1)}, bf16[512,128]{1,0:T(8,128)(2,1)}, bf16[128,512]{1,0:T(8,128)(2,1)}), (bf16[512,128]{1,0:T(8,128)(2,1)}, bf16[512,128]{1,0:T(8,128)(2,1)}, ...) | async-done | bytes 524304 | tf_op jit(solution)/shard_map/psum | solution.py:282
  600.3 25.5 %reduce-scatter.11.cloned.1.call-done = bf16[512,512]{1,0:T(8,128)(2,1)} async-done(((bf16[2048,512]{1,0:T(8,128)(2,1)}), bf16[512,512]{1,0:T(8,128)(2,1)}) %reduce-scatter.11.cloned.1.call-update) | async-done | bytes 524304 | tf_op jit(solution)/shard_map/reduce_scatter | solution.py:270
  629.9 64.7 %all-reduce = (f32[512]{0:T(512)}, f32[512]{0:T(512)}) all-reduce(f32[512]{0:T(512)S(1)} %get-tuple-element.156, f32[512]{0:T(512)S(1)} %get-tuple-element.154), channel_id=1, replica_groups=mesh['expert'=32,'tensor'=4] {'expert','tensor'}, use_global_device_ids=true, to_apply=%region_24.25 | all-reduce | flops 1024 | bytes 8192 | tf_op jit(solution)/shard_map/psum | solution.py:287
  694.5 74.4 %all-reduce.5.cloned.1.call-done = f32[512,32]{0,1:T(8,128)} async-done(((f32[512,32]{0,1:T(8,128)}), f32[512,32]{0,1:T(8,128)}) %all-reduce.5.cloned.1.call-update) | async-done | bytes 65552 | tf_op jit(solution)/shard_map/psum | solution.py:287
  (261 shorter events, 166.7 us)
Async XLA Ops:
  7.2 218.1 %copy-start = (bf16[1,512,512]{2,1,0:T(8,128)(2,1)S(1)}, bf16[1,512,512]{2,1,0:T(8,128)(2,1)}, u32[]{:S(2)}) copy-start(bf16[1,512,512]{2,1,0:T(8,128)(2,1)} %param.26) | copy-start | bytes 1572868
  7.2 41.8 %copy-start.22 = (bf16[512,128]{1,0:T(8,128)(2,1)S(1)}, bf16[512,128]{1,0:T(8,128)(2,1)}, u32[]{:S(2)}) copy-start(bf16[512,128]{1,0:T(8,128)(2,1)} %param.22) | copy-start | bytes 393220
  7.2 44.2 %copy-start.24 = (bf16[512,128]{1,0:T(8,128)(2,1)S(1)}, bf16[512,128]{1,0:T(8,128)(2,1)}, u32[]{:S(2)}) copy-start(bf16[512,128]{1,0:T(8,128)(2,1)} %param.21) | copy-start | bytes 393220
  7.2 39.2 %all-gather.5.cloned.1.call-start = ((), (), s32[]{:S(2)}) async-start(), calls=%async_computation.8 | async-start | bytes 2621440 | tf_op jit(solution)/shard_map/all_gather | solution.py:131
  8.5 44.5 %copy-start.30 = (f32[512]{0:T(512)}, f32[512]{0:T(512)S(1)}, u32[]{:S(2)}) copy-start(f32[512]{0:T(512)S(1)} %broadcast_multiply_fusion.5) | copy-start | bytes 6148
  9.9 43.2 %copy-start.33 = (f32[512]{0:T(512)}, f32[512]{0:T(512)S(1)}, u32[]{:S(2)}) copy-start(f32[512]{0:T(512)S(1)} %add_rsqrt_fusion.1) | copy-start | bytes 6148
  12.0 130.9 %reduce-scatter.5.cloned.1.call-start = ((), (), s32[]{:S(2)}) async-start(), calls=%async_computation.9 | async-start | bytes 2621440 | tf_op jit(solution)/shard_map/reduce_scatter | solution.py:145
  53.1 57.8 %copy-start.26 = (bf16[128,512]{1,0:T(8,128)(2,1)S(1)}, bf16[128,512]{1,0:T(8,128)(2,1)}, u32[]{:S(2)}) copy-start(bf16[128,512]{1,0:T(8,128)(2,1)} %param.24) | copy-start | bytes 393220
  109.5 33.4 %copy-start.4 = (bf16[512,512]{1,0:T(8,128)(2,1)S(1)}, bf16[512,512]{1,0:T(8,128)(2,1)}, u32[]{:S(2)}) copy-start(bf16[512,512]{1,0:T(8,128)(2,1)} %param.18) | copy-start | bytes 1572868
  109.9 35.6 %copy-start.35 = (f32[512]{0:T(512)S(1)}, f32[512]{0:T(512)}, u32[]{:S(2)}) copy-start(f32[512]{0:T(512)} %param.20) | copy-start | bytes 6148
  110.9 36.0 %copy-start.28 = (bf16[512,32]{0,1:T(8,128)(2,1)S(1)}, bf16[512,32]{0,1:T(8,128)(2,1)}, u32[]{:S(2)}) copy-start(bf16[512,32]{0,1:T(8,128)(2,1)} %param.25) | copy-start | bytes 98308
  112.9 34.3 %copy-start.32 = (s32[16,32]{1,0:T(8,128)S(1)}, s32[16,32]{1,0:T(8,128)}, u32[]{:S(2)}) copy-start(s32[16,32]{1,0:T(8,128)} %param.30) | copy-start | bytes 6148
  113.0 66.5 %all-gather.7.cloned.1.call-start = ((), (), s32[]{:S(2)}) async-start(), calls=%async_computation.10 | async-start | bytes 2621440 | tf_op jit(solution)/shard_map/all_gather | solution.py:171
  146.9 182.4 %copy-start.5 = (bf16[512,512]{1,0:T(8,128)(2,1)}, bf16[512,512]{1,0:T(8,128)(2,1)S(1)}, u32[]{:S(2)}) copy-start(bf16[512,512]{1,0:T(8,128)(2,1)S(1)} %multiply_convert_fusion.3) | copy-start | bytes 1572868
  148.8 63.9 %all-gather.9.cloned.1.call-start = ((), (), s32[]{:S(2)}) async-start(), calls=%async_computation.12 | async-start | bytes 2621440 | tf_op jit(solution)/shard_map/all_gather | solution.py:201
  183.6 36.4 %all-to-all-start = ((bf16[32,64,512]{2,1,0:T(8,128)(2,1)}), bf16[32,64,512]{2,1,0:T(8,128)(2,1)}, u32[]{:S(2)}, u32[]{:S(2)}) async-start(bf16[32,64,512]{2,1,0:T(8,128)(2,1)} %copy.64), calls=%async_computation.1 | async-start | bytes 4194304 | tf_op jit(solution)/shard_map/all_to_all | solution.py:172
  220.0 33.7 %all-to-all-start.2 = ((bf16[32,64,512]{2,1,0:T(8,128)(2,1)}), bf16[32,64,512]{2,1,0:T(8,128)(2,1)}, u32[]{:S(2)}, u32[]{:S(2)}) async-start(bf16[32,64,512]{2,1,0:T(8,128)(2,1)} %copy.67), calls=%async_computation.4 | async-start | bytes 4194304 | tf_op jit(solution)/shard_map/all_to_all | solution.py:202
  225.2 104.0 %reduce-scatter.9.cloned.1.call-start = ((), (), s32[]{:S(2)}) async-start(), calls=%async_computation.13 | async-start | bytes 2621440 | tf_op jit(solution)/shard_map/reduce_scatter | solution.py:222
  261.6 32.7 %copy-start.39 = (bf16[1,512,512]{2,1,0:T(8,128)(2,1)S(1)}, bf16[1,512,512]{2,1,0:T(8,128)(2,1)}, u32[]{:S(2)}) copy-start(bf16[1,512,512]{2,1,0:T(8,128)(2,1)} %param.27) | copy-start | bytes 1572868
  294.2 61.3 %reduce-scatter.7.cloned.1.call-start = ((), (), s32[]{:S(2)}) async-start(), calls=%async_computation.11 | async-start | bytes 2621440 | tf_op jit(solution)/shard_map/reduce_scatter | solution.py:186
  329.1 29.8 %copy-start.7 = (bf16[512,512]{1,0:T(8,128)(2,1)S(1)}, bf16[512,512]{1,0:T(8,128)(2,1)}, u32[]{:S(2)}) copy-start(bf16[512,512]{1,0:T(8,128)(2,1)} %reduce-scatter.5.cloned.1.call-done) | copy-start | bytes 1572868
  329.1 64.3 %all-gather.11.cloned.1.call-start = ((), (), s32[]{:S(2)}) async-start(), calls=%async_computation.14 | async-start | bytes 2621440 | tf_op jit(solution)/shard_map/all_gather | solution.py:242
  331.5 27.5 %copy-start.29 = (bf16[512,32]{0,1:T(8,128)(2,1)S(1)}, bf16[512,32]{0,1:T(8,128)(2,1)}, u32[]{:S(2)}) copy-start(bf16[512,32]{0,1:T(8,128)(2,1)} %param.25) | copy-start | bytes 98308
  360.3 33.1 %copy-start.27 = (bf16[128,512]{1,0:T(8,128)(2,1)S(1)}, bf16[128,512]{1,0:T(8,128)(2,1)}, u32[]{:S(2)}) copy-start(bf16[128,512]{1,0:T(8,128)(2,1)} %param.24) | copy-start | bytes 393220
  362.7 231.1 %all-reduce.7.cloned.1.call-start = ((), (), s32[]{:S(2)}) async-start(), calls=%async_computation.17 | async-start | bytes 1048576 | tf_op jit(solution)/shard_map/psum | solution.py:282
  490.2 135.5 %reduce-scatter.11.cloned.1.call-start = ((), (), s32[]{:S(2)}) async-start(), calls=%async_computation.15 | async-start | bytes 2621440 | tf_op jit(solution)/shard_map/reduce_scatter | solution.py:270
  495.8 273.1 %all-reduce.5.cloned.1.call-start = ((), (), s32[]{:S(2)}) async-start(), calls=%async_computation.16 | async-start | bytes 131072 | tf_op jit(solution)/shard_map/psum | solution.py:287
  500.5 125.2 %copy-start.31 = (f32[512]{0:T(512)S(1)}, f32[512]{0:T(512)}, u32[]{:S(2)}) copy-start(f32[512]{0:T(512)} %copy-done.30) | copy-start | bytes 6148
  500.5 125.2 %copy-start.34 = (f32[512]{0:T(512)S(1)}, f32[512]{0:T(512)}, u32[]{:S(2)}) copy-start(f32[512]{0:T(512)} %copy-done.33) | copy-start | bytes 6148
  500.5 125.2 %copy-start.37 = (f32[512]{0:T(512)S(1)}, f32[512]{0:T(512)}, u32[]{:S(2)}) copy-start(f32[512]{0:T(512)} %param.19) | copy-start | bytes 6148
  500.5 126.9 %copy-start.12 = (f32[512,512]{1,0:T(8,128)S(1)}, f32[512,512]{1,0:T(8,128)}, u32[]{:S(2)}) copy-start(f32[512,512]{1,0:T(8,128)} %get-tuple-element.205) | copy-start | bytes 3145732
  500.6 269.9 %copy-start.1 = (bf16[1,512,512]{2,1,0:T(8,128)(2,1)S(1)}, bf16[1,512,512]{2,1,0:T(8,128)(2,1)}, u32[]{:S(2)}) copy-start(bf16[1,512,512]{2,1,0:T(8,128)(2,1)} %param.26) | copy-start | bytes 1572868
  (34 other events, 105.9 us)
Sparse Core Ops, SparseCore 0:
  12.1 34.2 all-gather.4
  113.1 29.8 reduce-scatter.4
  148.9 30.5 all-gather.6
  181.7 30.9 all-gather.8
  294.3 26.2 reduce-scatter.8
  329.3 26.2 reduce-scatter.6
  362.8 30.5 all-gather.10
  490.3 103.3 all-reduce.6
  596.2 29.5 reduce-scatter.10
  631.6 137.2 all-reduce.4
where the time goes:
time: 788 us; the launch traced here: 778 us
  waiting for transfers between devices  381 us (48%)
  matrix products  132 us (17%)
  blocking collectives  129 us (16%)
  other arithmetic  62.2 us (8%)
  local copies, waits for them, and re-layouts  27.2 us (3%)
  loops' own time  16.4 us (2%)
  between operations  15.1 us (2%)
  starting transfers between devices  13.9 us (2%)
    psum x1, waiting for transfers between devices, body(): lax.psum(query_part.astype(jnp.bfloat16), 'expert').astype(jnp.float32)  88.3 us
    psum x1, waiting for transfers between devices, body(): lax.psum((first_part, second_part, router_part), ('expert', 'tensor'))  74.4 us
    psum x1, blocking collectives, body(): lax.psum((first_part, second_part, router_part), ('expert', 'tensor'))  64.7 us
    all_gather x1, waiting for transfers between devices, body(): lax.all_gather(normed_one.astype(jnp.bfloat16), 'tensor', axis=0, tiled=T...  33.8 us
    all_to_all x1, blocking collectives, body(): lax.all_to_all(to_homes(grad_part, expert_size).astype(jnp.bfloat16), 'ex...  32.6 us
    all_to_all x1, blocking collectives, body(): lax.all_to_all(to_homes(part_out, expert_size).astype(jnp.bfloat16), 'exp...  32 us
    all_gather x1, waiting for transfers between devices, body(): lax.all_gather(grad_residual.astype(jnp.bfloat16), 'tensor', axis=0, tile...  30.5 us
    reduce_scatter x1, waiting for transfers between devices, body(): lax.psum_scatter(jnp.dot(context, output_weight, preferred_element_type=j...  29.8 us
  transfers between devices with their start and end apart: 12, of which 11 were waited for; matrix products, arithmetic and copies ran while one was open for 6% of the time, Pallas kernels for 0%

commit v1 on v0

--- a/solution.py
+++ b/solution.py
@@ -2,6 +2,7 @@
 import jax.numpy as jnp
 from jax import lax
 from jax.sharding import PartitionSpec as P
+from jax.lax import psum
 
 HEAD_DIM = 64
 GROUP = 32
@@ -284,8 +285,8 @@
         lax.psum(value_part.astype(jnp.bfloat16), "expert").astype(jnp.float32),
         lax.psum(output_part.astype(jnp.bfloat16), "expert").astype(jnp.float32),
     )
-    first_gain_grad, second_gain_grad, router_grad = lax.psum(
-        (first_part, second_part, router_part), ("expert", "tensor")
+    first_gain_grad, second_gain_grad, router_grad = psum(
+        psum((first_part, second_part, router_part), axis_name="tensor"), axis_name="expert"
     )
     return (
         layer_output,

time: 788 us -> 743 us (0.943)
  waiting for transfers between devices: 381 us -> 329 us
    psum x1 -> x2, waiting for transfers between devices: 74.4 us -> 22.7 us  [the longest x1 22.7 us: body(): psum(psum((first_part, second_part, router_part), axis_name='tensor'), ax...]
    psum x1 -> x2, blocking collectives: 64.7 us -> 71.7 us  [the longest x1 65.2 us: body(): psum(psum((first_part, second_part, router_part), axis_name='tensor'), ax...]
  transfers between devices with their start and end apart: 12 -> 13, of which waited for: 11 -> 11; matrix products, arithmetic and copies ran while one was open for 6% -> 19% of each run, Pallas kernels for 0% -> 0%
where the time goes in v1:
time: 743 us; the launch traced here: 732 us
  waiting for transfers between devices  329 us (44%)
  blocking collectives  136 us (18%)
  matrix products  132 us (18%)
  other arithmetic  62.2 us (8%)
  local copies, waits for them, and re-layouts  28 us (4%)
  loops' own time  16.4 us (2%)
  between operations  14.8 us (2%)
  starting transfers between devices  13.9 us (2%)
    psum x1, waiting for transfers between devices, body(): lax.psum(query_part.astype(jnp.bfloat16), 'expert').astype(jnp.float32)  89.3 us
    psum x1, blocking collectives, body(): psum(psum((first_part, second_part, router_part), axis_name='tensor'), ax...  65.2 us
    all_gather x1, waiting for transfers between devices, body(): lax.all_gather(normed_one.astype(jnp.bfloat16), 'tensor', axis=0, tiled=T...  33.8 us
    all_to_all x1, blocking collectives, body(): lax.all_to_all(to_homes(grad_part, expert_size).astype(jnp.bfloat16), 'ex...  32.5 us
    all_to_all x1, blocking collectives, body(): lax.all_to_all(to_homes(part_out, expert_size).astype(jnp.bfloat16), 'exp...  32.1 us
    reduce_scatter x1, waiting for transfers between devices, body(): lax.psum_scatter(jnp.dot(context, output_weight, preferred_element_type=j...  29.8 us
    all_gather x1, waiting for transfers between devices, body(): lax.all_gather(grad_residual.astype(jnp.bfloat16), 'tensor', axis=0, tile...  29.5 us
    all_gather x1, waiting for transfers between devices, body(): sequence_mix = lax.all_gather(mixed_rows, 'tensor', axis=1, tiled=True)  27.4 us
  transfers between devices with their start and end apart: 13, of which 11 were waited for; matrix products, arithmetic and copies ran while one was open for 19% of the time, Pallas kernels for 0%

profile of v1, /device:TPU:1, one launch (start us, length us, event | category | flops | bytes accessed | tf_op | source)
XLA Modules:
  0.0 732.3 jit_solution(5763961517404616485)
XLA Ops:
  12.6 33.8 %all-gather.5.cloned.1.call-done = bf16[2048,512]{1,0:T(8,128)(2,1)} async-done(((bf16[512,512]{1,0:T(8,128)(2,1)}), bf16[2048,512]{1,0:T(8,128)(2,1)}) %all-gather.5.cloned.1.call-update) | async-done | bytes 2097168 | tf_op jit(solution)/shard_map/all_gather | solution.py:132
  53.1 56.4 %while.27 = (s32[]{:T(128)}, bf16[4,512,2,64]{1,3,2,0:T(8,128)(2,1)S(1)}, f32[4,2,512]{2,1,0:T(2,128)}, s32[4]{0:T(128)}, s32[]{:T(128)}, /*index=5*/bf16[2048,2...) while((s32[]{:T(128)}, ...), condition=%wide.region_5.6_spmd, body=%wide.region_2.5_spmd.sunk | while | flops 564200960 | bytes 30711992 | solution.py:53
  58.4 3.1 fusion.162
  72.5 3.1 fusion.162
  113.2 29.8 %reduce-scatter.5.cloned.1.call-done = bf16[512,512]{1,0:T(8,128)(2,1)} async-done(((bf16[2048,512]{1,0:T(8,128)(2,1)}), bf16[512,512]{1,0:T(8,128)(2,1)}) %reduce-scatter.5.cloned.1.call-update) | async-done | bytes 524304 | tf_op jit(solution)/shard_map/reduce_scatter | solution.py:146
  152.1 27.4 %all-gather.7.cloned.1.call-done = bf16[32,64,512]{2,0,1:T(8,128)(2,1)} async-done(((bf16[32,16,512]{2,0,1:T(8,128)(2,1)}), bf16[32,64,512]{2,0,1:T(8,128)(2,1)}) %all-gather.7.cloned.1.call-update) | async-done | bytes 2097168 | tf_op jit(solution)/shard_map/all_gather | solution.py:172
  179.5 4.1 copy.64
  183.6 8.1 %all-to-all-start = ((bf16[32,64,512]{2,1,0:T(8,128)(2,1)}), bf16[32,64,512]{2,1,0:T(8,128)(2,1)}, u32[]{:S(2)}, u32[]{:S(2)}) async-start(bf16[32,64,512]{2,1,0:T(8,128)(2,1)} %copy.64), calls=%async_computation.1 | async-start | bytes 4194304 | tf_op jit(solution)/shard_map/all_to_all | solution.py:173
  191.6 21.0 %all-gather.9.cloned.1.call-done = bf16[32,64,512]{2,0,1:T(8,128)(2,1)} async-done(((bf16[32,16,512]{2,0,1:T(8,128)(2,1)}), bf16[32,64,512]{2,0,1:T(8,128)(2,1)}) %all-gather.9.cloned.1.call-update) | async-done | bytes 2097168 | tf_op jit(solution)/shard_map/all_gather | solution.py:202
  212.7 4.1 copy.67
  216.8 3.2 all-to-all-done
  220.0 5.2 all-to-all-start.2
  225.3 6.0 multiply_convert_fusion.2
  231.3 22.3 %all-to-all-done.2 = bf16[32,64,512]{2,1,0:T(8,128)(2,1)} async-done(((bf16[32,64,512]{2,1,0:T(8,128)(2,1)}), bf16[32,64,512]{2,1,0:T(8,128)(2,1)}, u32[]{:S(2)}, u32[]{:S(2)}) %all-to-all-start.2) | async-done | bytes 2097184 | tf_op jit(solution)/shard_map/all_to_all | solution.py:203
  253.7 5.1 multiply_convert_fusion.1
  261.4 32.5 %all_to_all.28 = bf16[32,64,512]{2,1,0:T(8,128)(2,1)} all-to-all(bf16[32,64,512]{2,1,0:T(8,128)(2,1)S(1)} %convolution_convert_fusion.5), channel_id=1, replica_groups=mesh['expert'=32,'tensor'=4] {'expert'}, dimensions={0} | all-to-all | bytes 4194304 | tf_op jit(solution)/shard_map/all_to_all | solution.py:216
  296.8 32.1 %all_to_all.29 = bf16[32,64,512]{2,1,0:T(8,128)(2,1)} all-to-all(bf16[32,64,512]{2,1,0:T(8,128)(2,1)S(1)} %convolution_convert_fusion.6), channel_id=1, replica_groups=mesh['expert'=32,'tensor'=4] {'expert'}, dimensions={0} | all-to-all | bytes 4194304 | tf_op jit(solution)/shard_map/all_to_all | solution.py:180
  331.3 24.1 %reduce-scatter.7.cloned.1.call-done = bf16[32,16,512]{2,1,0:T(8,128)(2,1)} async-done(((bf16[32,64,512]{2,1,0:T(8,128)(2,1)}), bf16[32,16,512]{2,1,0:T(8,128)(2,1)}) %reduce-scatter.7.cloned.1.call-update) | async-done | bytes 524304 | tf_op jit(solution)/shard_map/reduce_scatter | solution.py:187
  363.7 29.5 %all-gather.11.cloned.1.call-done = bf16[2048,512]{1,0:T(8,128)(2,1)} async-done(((bf16[512,512]{1,0:T(8,128)(2,1)}), bf16[2048,512]{1,0:T(8,128)(2,1)}) %all-gather.11.cloned.1.call-update) | async-done | bytes 2097168 | tf_op jit(solution)/shard_map/all_gather | solution.py:243
  395.7 81.7 %while.28 = (s32[]{:T(128)}, f32[2048,2,64]{0,2,1:T(8,128)S(1)}, f32[2048,2,64]{0,2,1:T(8,128)}, bf16[4,512,2,64]{1,3,2,0:T(8,128)(2,1)}, s32[4]{0:T(128)}, /*in...) while((s32[]{:T(128)}, f32[2048,2,64]{0,2,1:T(8,128)S(1)}, ...), condition=%wide.region_19.20_spmd.clone, body=%wide.region_17.19_spmd.clone.sunk | while | flops 1377109504 | bytes 86282592 | solution.py:88
  406.7 3.2 multiply_reduce_fusion.7
  427.1 3.2 multiply_reduce_fusion.7
  447.5 3.2 multiply_reduce_fusion.7
  467.8 3.2 multiply_reduce_fusion.7
  490.1 5.5 add_convert_fusion
  495.7 4.6 convolution_bitcast_fusion
  500.4 4.0 convolution_bitcast_fusion.1
  504.4 89.3 %all-reduce.11.cloned.1.call-done = (bf16[512,128]{1,0:T(8,128)(2,1)}, bf16[512,128]{1,0:T(8,128)(2,1)}, bf16[512,128]{1,0:T(8,128)(2,1)}, bf16[128,512]{1,0:T(8,128)(2,1)}) async-done(((bf16[512,128]{1,0:T(8,128)(2,1)}, bf16[512,128]{1,0:T(8,128)(2,1)}, bf16[512,128]{1,0:T(8,128)(2,1)}, bf16[128,512]{1,0:T(8,128)(2,1)}), (bf16[512,128]{1,0:T(8,128)(2,1)}, bf16[512,128]{1,0:T(8,128)(2,1)}, ...) | async-done | bytes 524304 | tf_op jit(solution)/shard_map/psum | solution.py:283
  600.1 25.4 %reduce-scatter.11.cloned.1.call-done = bf16[512,512]{1,0:T(8,128)(2,1)} async-done(((bf16[2048,512]{1,0:T(8,128)(2,1)}), bf16[512,512]{1,0:T(8,128)(2,1)}) %reduce-scatter.11.cloned.1.call-update) | async-done | bytes 524304 | tf_op jit(solution)/shard_map/reduce_scatter | solution.py:271
  629.7 6.5 all-reduce.1
  636.2 65.2 %all-reduce = (f32[512]{0:T(512)}, f32[512]{0:T(512)}) all-reduce(f32[512]{0:T(512)S(1)} %get-tuple-element.200, f32[512]{0:T(512)S(1)} %get-tuple-element.201), channel_id=1, replica_groups=mesh['expert'=32,'tensor'=4] {'expert'}, use_global_device_ids=true, to_apply=%region_25.26 | all-reduce | flops 1024 | bytes 8192 | tf_op jit(solution)/shard_map/psum | solution.py:288
  701.4 22.7 %all-reduce.9.cloned.1.call-done = f32[512,32]{0,1:T(8,128)} async-done(((f32[512,32]{0,1:T(8,128)}), f32[512,32]{0,1:T(8,128)}) %all-reduce.9.cloned.1.call-update) | async-done | bytes 65552 | tf_op jit(solution)/shard_map/psum | solution.py:288
  (269 shorter events, 170.6 us)
Async XLA Ops:
  7.2 218.1 %copy-start = (bf16[1,512,512]{2,1,0:T(8,128)(2,1)S(1)}, bf16[1,512,512]{2,1,0:T(8,128)(2,1)}, u32[]{:S(2)}) copy-start(bf16[1,512,512]{2,1,0:T(8,128)(2,1)} %param.26) | copy-start | bytes 1572868
  7.2 41.8 %copy-start.24 = (bf16[512,128]{1,0:T(8,128)(2,1)S(1)}, bf16[512,128]{1,0:T(8,128)(2,1)}, u32[]{:S(2)}) copy-start(bf16[512,128]{1,0:T(8,128)(2,1)} %param.22) | copy-start | bytes 393220
  7.2 44.2 %copy-start.26 = (bf16[512,128]{1,0:T(8,128)(2,1)S(1)}, bf16[512,128]{1,0:T(8,128)(2,1)}, u32[]{:S(2)}) copy-start(bf16[512,128]{1,0:T(8,128)(2,1)} %param.21) | copy-start | bytes 393220
  7.2 39.2 %all-gather.5.cloned.1.call-start = ((), (), s32[]{:S(2)}) async-start(), calls=%async_computation.8 | async-start | bytes 2621440 | tf_op jit(solution)/shard_map/all_gather | solution.py:132
  8.5 44.5 %copy-start.32 = (f32[512]{0:T(512)}, f32[512]{0:T(512)S(1)}, u32[]{:S(2)}) copy-start(f32[512]{0:T(512)S(1)} %broadcast_multiply_fusion.5) | copy-start | bytes 6148
  9.9 43.2 %copy-start.35 = (f32[512]{0:T(512)}, f32[512]{0:T(512)S(1)}, u32[]{:S(2)}) copy-start(f32[512]{0:T(512)S(1)} %add_rsqrt_fusion.1) | copy-start | bytes 6148
  12.0 130.9 %reduce-scatter.5.cloned.1.call-start = ((), (), s32[]{:S(2)}) async-start(), calls=%async_computation.9 | async-start | bytes 2621440 | tf_op jit(solution)/shard_map/reduce_scatter | solution.py:146
  53.1 57.8 %copy-start.28 = (bf16[128,512]{1,0:T(8,128)(2,1)S(1)}, bf16[128,512]{1,0:T(8,128)(2,1)}, u32[]{:S(2)}) copy-start(bf16[128,512]{1,0:T(8,128)(2,1)} %param.24) | copy-start | bytes 393220
  109.5 33.4 %copy-start.4 = (bf16[512,512]{1,0:T(8,128)(2,1)S(1)}, bf16[512,512]{1,0:T(8,128)(2,1)}, u32[]{:S(2)}) copy-start(bf16[512,512]{1,0:T(8,128)(2,1)} %param.18) | copy-start | bytes 1572868
  109.9 35.6 %copy-start.37 = (f32[512]{0:T(512)S(1)}, f32[512]{0:T(512)}, u32[]{:S(2)}) copy-start(f32[512]{0:T(512)} %param.20) | copy-start | bytes 6148
  110.8 36.0 %copy-start.30 = (bf16[512,32]{0,1:T(8,128)(2,1)S(1)}, bf16[512,32]{0,1:T(8,128)(2,1)}, u32[]{:S(2)}) copy-start(bf16[512,32]{0,1:T(8,128)(2,1)} %param.25) | copy-start | bytes 98308
  112.9 34.3 %copy-start.34 = (s32[16,32]{1,0:T(8,128)S(1)}, s32[16,32]{1,0:T(8,128)}, u32[]{:S(2)}) copy-start(s32[16,32]{1,0:T(8,128)} %param.30) | copy-start | bytes 6148
  112.9 66.5 %all-gather.7.cloned.1.call-start = ((), (), s32[]{:S(2)}) async-start(), calls=%async_computation.10 | async-start | bytes 2621440 | tf_op jit(solution)/shard_map/all_gather | solution.py:172
  146.8 182.2 %copy-start.5 = (bf16[512,512]{1,0:T(8,128)(2,1)}, bf16[512,512]{1,0:T(8,128)(2,1)S(1)}, u32[]{:S(2)}) copy-start(bf16[512,512]{1,0:T(8,128)(2,1)S(1)} %multiply_convert_fusion.3) | copy-start | bytes 1572868
  148.8 63.9 %all-gather.9.cloned.1.call-start = ((), (), s32[]{:S(2)}) async-start(), calls=%async_computation.12 | async-start | bytes 2621440 | tf_op jit(solution)/shard_map/all_gather | solution.py:202
  183.6 36.4 %all-to-all-start = ((bf16[32,64,512]{2,1,0:T(8,128)(2,1)}), bf16[32,64,512]{2,1,0:T(8,128)(2,1)}, u32[]{:S(2)}, u32[]{:S(2)}) async-start(bf16[32,64,512]{2,1,0:T(8,128)(2,1)} %copy.64), calls=%async_computation.1 | async-start | bytes 4194304 | tf_op jit(solution)/shard_map/all_to_all | solution.py:173
  220.0 33.7 %all-to-all-start.2 = ((bf16[32,64,512]{2,1,0:T(8,128)(2,1)}), bf16[32,64,512]{2,1,0:T(8,128)(2,1)}, u32[]{:S(2)}, u32[]{:S(2)}) async-start(bf16[32,64,512]{2,1,0:T(8,128)(2,1)} %copy.67), calls=%async_computation.4 | async-start | bytes 4194304 | tf_op jit(solution)/shard_map/all_to_all | solution.py:203
  225.2 103.8 %reduce-scatter.9.cloned.1.call-start = ((), (), s32[]{:S(2)}) async-start(), calls=%async_computation.13 | async-start | bytes 2621440 | tf_op jit(solution)/shard_map/reduce_scatter | solution.py:223
  293.9 61.5 %reduce-scatter.7.cloned.1.call-start = ((), (), s32[]{:S(2)}) async-start(), calls=%async_computation.11 | async-start | bytes 2621440 | tf_op jit(solution)/shard_map/reduce_scatter | solution.py:187
  296.8 58.6 %copy-start.10 = (bf16[512,512]{1,0:T(8,128)(2,1)S(1)}, bf16[512,512]{1,0:T(8,128)(2,1)}, u32[]{:S(2)}) copy-start(bf16[512,512]{1,0:T(8,128)(2,1)} %copy-done.9) | copy-start | bytes 1572868
  328.9 29.8 %copy-start.7 = (bf16[512,512]{1,0:T(8,128)(2,1)S(1)}, bf16[512,512]{1,0:T(8,128)(2,1)}, u32[]{:S(2)}) copy-start(bf16[512,512]{1,0:T(8,128)(2,1)} %reduce-scatter.5.cloned.1.call-done) | copy-start | bytes 1572868
  329.0 64.3 %all-gather.11.cloned.1.call-start = ((), (), s32[]{:S(2)}) async-start(), calls=%async_computation.14 | async-start | bytes 2621440 | tf_op jit(solution)/shard_map/all_gather | solution.py:243
  360.6 32.6 %copy-start.29 = (bf16[128,512]{1,0:T(8,128)(2,1)S(1)}, bf16[128,512]{1,0:T(8,128)(2,1)}, u32[]{:S(2)}) copy-start(bf16[128,512]{1,0:T(8,128)(2,1)} %param.24) | copy-start | bytes 393220
  362.5 141.8 %all-reduce.7.cloned.1.call-start = ((), (), s32[]{:S(2)}) async-start(), calls=%async_computation.16 | async-start | bytes 131072 | tf_op jit(solution)/shard_map/psum | solution.py:289
  363.5 230.1 %all-reduce.11.cloned.1.call-start = ((), (), s32[]{:S(2)}) async-start(), calls=%async_computation.18 | async-start | bytes 1048576 | tf_op jit(solution)/shard_map/psum | solution.py:283
  490.0 135.5 %reduce-scatter.11.cloned.1.call-start = ((), (), s32[]{:S(2)}) async-start(), calls=%async_computation.15 | async-start | bytes 2621440 | tf_op jit(solution)/shard_map/reduce_scatter | solution.py:271
  495.7 228.4 %all-reduce.9.cloned.1.call-start = ((), (), s32[]{:S(2)}) async-start(), calls=%async_computation.17 | async-start | bytes 131072 | tf_op jit(solution)/shard_map/psum | solution.py:288
  500.3 125.2 %copy-start.33 = (f32[512]{0:T(512)S(1)}, f32[512]{0:T(512)}, u32[]{:S(2)}) copy-start(f32[512]{0:T(512)} %copy-done.32) | copy-start | bytes 6148
  500.3 125.2 %copy-start.36 = (f32[512]{0:T(512)S(1)}, f32[512]{0:T(512)}, u32[]{:S(2)}) copy-start(f32[512]{0:T(512)} %copy-done.35) | copy-start | bytes 6148
  500.3 125.2 %copy-start.39 = (f32[512]{0:T(512)S(1)}, f32[512]{0:T(512)}, u32[]{:S(2)}) copy-start(f32[512]{0:T(512)} %param.19) | copy-start | bytes 6148
  500.4 126.9 %copy-start.14 = (f32[512,512]{1,0:T(8,128)S(1)}, f32[512,512]{1,0:T(8,128)}, u32[]{:S(2)}) copy-start(f32[512,512]{1,0:T(8,128)} %get-tuple-element.207) | copy-start | bytes 3145732
  500.4 225.2 %copy-start.1 = (bf16[1,512,512]{2,1,0:T(8,128)(2,1)S(1)}, bf16[1,512,512]{2,1,0:T(8,128)(2,1)}, u32[]{:S(2)}) copy-start(bf16[1,512,512]{2,1,0:T(8,128)(2,1)} %param.26) | copy-start | bytes 1572868
  (37 other events, 158.9 us)
Sparse Core Ops, SparseCore 0:
  12.1 34.2 all-gather.4
  113.1 29.8 reduce-scatter.4
  148.9 30.5 all-gather.6
  181.7 30.9 all-gather.8
  294.0 26.2 reduce-scatter.8
  329.1 26.2 reduce-scatter.6
  362.6 30.5 all-gather.10
  396.2 38.9 all-reduce.6
  490.2 103.4 all-reduce.10
  596.0 29.5 reduce-scatter.10
  628.8 95.1 all-reduce.8
